TPU v7x, 128 devices: a whole 4x4x4 slice. The times are simulated.
128 devices in a mesh: dp: 64 (over x, z_hi, y, core), tensor: 2 (over z_lo).
Axes of the slice: x: 4, y: 4, z: 4 (z_hi: 2, z_lo: 2; z = z_hi * 2 + z_lo), core: 2. Of those that a mesh axis runs over, the one named last changes fastest.
Arguments:
- inputs: bfloat16 [16384, 1152], P(('dp', 'tensor')), may hold values from -24 to 24
- doc_ids: int32 [64, 256], P('dp'), may hold values from 0 to 3, never falling along the last dimension, each value on 1 to 128 neighbouring positions
- prenorm: bfloat16 [1152], P('dp'), may hold values from 0.099609375 to 1.8984375
- query_proj: bfloat16 [1152, 1024], P('dp', 'tensor'), may hold values from -0.1875 to 0.1875
- key_proj: bfloat16 [1152, 256], P('dp'), may hold values from -0.1875 to 0.1875
- value_proj: bfloat16 [1152, 256], P('dp'), may hold values from -0.1875 to 0.1875
- querynorm: bfloat16 [256], P('dp'), may hold values from 0.5 to 2
- keynorm: bfloat16 [256], P('dp'), may hold values from 0.5 to 2
- output_proj: bfloat16 [1024, 1152], P('tensor', 'dp'), may hold values from -0.1875 to 0.1875
- postnorm: bfloat16 [1152], P('dp'), may hold values from 0.099609375 to 1.8984375
- ffnnorm: bfloat16 [1152], P('dp'), may hold values from 0.099609375 to 1.8984375
- gate_proj: bfloat16 [1152, 6912], P('dp', 'tensor'), may hold values from -0.1875 to 0.1875
- up_proj: bfloat16 [1152, 6912], P('dp', 'tensor'), may hold values from -0.1875 to 0.1875
- down_proj: bfloat16 [6912, 1152], P('tensor', 'dp'), may hold values from -0.078125 to 0.078125
- endnorm: bfloat16 [1152], P('dp'), may hold values from 0.099609375 to 1.8984375
- cotangent: bfloat16 [16384, 1152], P(('dp', 'tensor')), may hold values from -24 to 24
Outputs:
- layer_out: bfloat16 [16384, 1152], P(('dp', 'tensor'))
- inputs_grad: float32 [16384, 1152], P(('dp', 'tensor'))
- prenorm_grad: float32 [1152], P('dp')
- query_grad: float32 [1152, 1024], P('dp', 'tensor')
- key_grad: float32 [1152, 256], P('dp')
- value_grad: float32 [1152, 256], P('dp')
- querynorm_grad: float32 [256], P('dp')
- keynorm_grad: float32 [256], P('dp')
- output_grad: float32 [1024, 1152], P('tensor', 'dp')
- postnorm_grad: float32 [1152], P('dp')
- ffnnorm_grad: float32 [1152], P('dp')
- gate_grad: float32 [1152, 6912], P('dp', 'tensor')
- up_grad: float32 [1152, 6912], P('dp', 'tensor')
- down_grad: float32 [6912, 1152], P('tensor', 'dp')
- endnorm_grad: float32 [1152], P('dp')
Inputs may be any that keep to these rules, and one draw needn't show every extreme that they name: `doc_ids`: in each sequence the document numbers never fall; every one of the 4 documents has 1 to half of 256 tokens, and some document has exactly half of 256 tokens.
All inputs are finite; a program needn't handle non-finite values.
Results may differ from a plain program's by a relative error of at most 0.025.
Values may be sent and summed in bfloat16 or wider, within the bound.
No kernel may reach another device: no remote copies, remote signals or barrier semaphores. Data moves between devices by JAX's collectives and lax.ppermute only.
A program may use at most 256 MiB of HBM per device.

v0:
```python
from functools import partial
import math
import jax
import jax.numpy as jnp
from jax import lax
from jax.sharding import PartitionSpec as P

H = 4
HD = 256
epsilon = 1e-06
rope_base = 1000000.0
query_scale = 0.0625


def sent_together(arrays, axis, dim, along):
    both = jnp.concatenate(arrays, axis=along)
    whole, at, gathered = (lax.all_gather(both, axis, axis=dim, tiled=True), 0, [])
    for a in arrays:
        gathered.append(lax.slice_in_dim(whole, at, at + a.shape[along], axis=along))
        at += a.shape[along]
    return tuple(gathered)


def gather_turned(arrays, axis, dims):
    turned = [jnp.moveaxis(a, dim, 0) for a, dim in zip(arrays, dims)]
    widths = [t[0].size for t in turned]
    both = jnp.concatenate([t.reshape(-1, w) for t, w in zip(turned, widths)], axis=1)
    whole = lax.all_gather(both, axis, axis=0, tiled=True)
    tiles = jnp.split(whole, [sum(widths[:k]) for k in range(1, len(widths))], axis=1)
    return tuple(
        (
            jnp.moveaxis(b.reshape(-1, *t.shape[1:]), 0, dim)
            for b, t, dim in zip(tiles, turned, dims)
        )
    )


def rms_scale(values, scales):
    mean_sq = jnp.mean(values * values, axis=-1, keepdims=True)
    return values * lax.rsqrt(mean_sq + epsilon) * scales


def head_piece(cos_tab, sin_tab, factor, raw_heads, scales):
    normed = rms_scale(raw_heads, scales)
    half_width = normed.shape[-1] // 2
    first_half = normed[..., :half_width]
    second = normed[..., half_width:]
    cos_rows = cos_tab[:, None, :]
    sin_rows = sin_tab[:, None, :]
    turned = jnp.concatenate(
        [first_half * cos_rows - second * sin_rows, second * cos_rows + first_half * sin_rows],
        axis=-1,
    )
    return turned * factor


def gelu_mix(gate_in, up_in):
    return jax.nn.gelu(gate_in, approximate=True) * up_in


def matmul(left_op, right_op):
    return jnp.dot(left_op, right_op, preferred_element_type=jnp.float32)


def matmul_nt(left_op, right_op):
    return lax.dot_general(
        left_op, right_op, (((1,), (1,)), ((), ())), preferred_element_type=jnp.float32
    )


def matmul_tn(left_op, right_op):
    return lax.dot_general(
        left_op, right_op, (((0,), (0,)), ((), ())), preferred_element_type=jnp.float32
    )


def rope_tables(segment):
    seq_length = segment.shape[0]
    token_index = jnp.arange(seq_length, dtype=jnp.int32)
    same_doc = segment[:, None] == segment[None, :]
    earlier = token_index[None, :] < token_index[:, None]
    position = jnp.sum(jnp.where(same_doc & earlier, 1, 0).astype(jnp.int32), axis=1).astype(
        jnp.float32
    )
    freq_rates = jnp.exp(jnp.arange(HD // 2, dtype=jnp.float32) * (-2.0 * math.log(rope_base) / HD))
    angles = position[:, None] * freq_rates[None, :]
    allowed = same_doc & (token_index[None, :] <= token_index[:, None])
    return (jnp.cos(angles), jnp.sin(angles), allowed)


def widen_rows(local_rows):
    return lax.all_gather(local_rows, "tensor", axis=0, tiled=True)


def narrow_rows(partial_rows):
    return lax.psum_scatter(partial_rows, "tensor", scatter_dimension=0, tiled=True)


def on_device(
    inputs,
    doc_ids,
    prenorm,
    query_proj,
    key_proj,
    value_proj,
    querynorm,
    keynorm,
    output_proj,
    postnorm,
    ffnnorm,
    gate_proj,
    up_proj,
    down_proj,
    endnorm,
    cotangent,
):
    tensor_size = lax.axis_size("tensor")
    local_heads = H // tensor_size
    seq_length = doc_ids.shape[1]
    kv_share = 1.0 / tensor_size
    width_rows = prenorm.shape[0]
    head_rows = querynorm.shape[0]
    attn_set = (
        *sent_together((query_proj, key_proj, value_proj), "dp", 0, 1),
        lax.all_gather(output_proj, "dp", axis=1, tiled=True),
        lax.all_gather(prenorm, "dp", axis=0, tiled=True),
        lax.all_gather(querynorm, "dp", axis=0, tiled=True),
        lax.all_gather(keynorm, "dp", axis=0, tiled=True),
        lax.all_gather(postnorm, "dp", axis=0, tiled=True),
    )
    ffn_set = ()
    query_all, key_all, value_all, out_all = (attn_set[0], attn_set[1], attn_set[2], attn_set[3])
    pre_gain = attn_set[4].astype(jnp.float32)
    qgain = attn_set[5].astype(jnp.float32)
    kgain = attn_set[6].astype(jnp.float32)
    post_gain = attn_set[7].astype(jnp.float32)
    cos_tab, sin_tab, allowed = rope_tables(doc_ids[0])
    mask_rows = jnp.repeat(allowed, local_heads, axis=0)
    resid = inputs.astype(jnp.float32)
    normed_f, in_back = jax.vjp(rms_scale, resid, pre_gain)
    normed_in = widen_rows(normed_f.astype(jnp.bfloat16))
    q_raw = matmul(normed_in, query_all).reshape(seq_length, local_heads, HD)
    k_raw = matmul(normed_in, key_all).reshape(seq_length, 1, HD)
    values_b = matmul(normed_in, value_all).astype(jnp.bfloat16)
    q_full, q_back = jax.vjp(partial(head_piece, cos_tab, sin_tab, query_scale), q_raw, qgain)
    k_full, k_back = jax.vjp(partial(head_piece, cos_tab, sin_tab, 1.0), k_raw, kgain)
    query_rows = q_full.astype(jnp.bfloat16).reshape(seq_length * local_heads, HD)
    keys_b = k_full[:, 0, :].astype(jnp.bfloat16)
    scores = matmul_nt(query_rows, keys_b)
    exp_scores = jnp.where(mask_rows, jnp.exp(scores), 0.0)
    log_total = jnp.log(jnp.sum(exp_scores, axis=1, keepdims=True))
    probs_b = jnp.where(mask_rows, jnp.exp(scores - log_total), 0.0).astype(jnp.bfloat16)
    mixed_rows = matmul(probs_b, values_b).astype(jnp.bfloat16)
    mixed = mixed_rows.reshape(seq_length, local_heads * HD)
    branch = narrow_rows(matmul(mixed, out_all))
    attn_norm, attn_back = jax.vjp(rms_scale, branch, post_gain)
    hidden = resid + attn_norm
    ffn_set = gather_turned(
        (gate_proj, up_proj, down_proj, ffnnorm, endnorm), "dp", (0, 0, 1, 0, 0)
    )
    gate_all, up_all, down_all = (ffn_set[0], ffn_set[1], ffn_set[2])
    ffn_gain = ffn_set[3].astype(jnp.float32)
    end_gain = ffn_set[4].astype(jnp.float32)
    ff_norm, ff_in_back = jax.vjp(rms_scale, hidden, ffn_gain)
    ff_input = widen_rows(ff_norm.astype(jnp.bfloat16))
    gate_f = matmul(ff_input, gate_all)
    up_f = matmul(ff_input, up_all)
    product, mix_back = jax.vjp(gelu_mix, gate_f, up_f)
    act = product.astype(jnp.bfloat16)
    ff_branch = narrow_rows(matmul(act, down_all))
    end_norm, end_back = jax.vjp(rms_scale, ff_branch, end_gain)
    layer_out = (hidden + end_norm).astype(jnp.bfloat16)
    grad_out = cotangent.astype(jnp.float32)
    d_ff, grad_end = end_back(grad_out)
    d_ff_rows = widen_rows(d_ff.astype(jnp.bfloat16))
    d_act = matmul_nt(d_ff_rows, down_all)
    d_gate, d_up = mix_back(d_act)
    d_gate_b = d_gate.astype(jnp.bfloat16)
    d_up_b = d_up.astype(jnp.bfloat16)
    hidden_cols = d_gate_b.shape[1]
    ff_sums = lax.psum_scatter(
        jnp.concatenate(
            [matmul_tn(ff_input, d_gate_b), matmul_tn(ff_input, d_up_b), matmul_tn(d_ff_rows, act)],
            axis=1,
        ),
        "dp",
        scatter_dimension=0,
        tiled=True,
    )
    sent_gate = ff_sums[:, :hidden_cols]
    sent_up = ff_sums[:, hidden_cols : 2 * hidden_cols]
    sent_down = ff_sums[:, 2 * hidden_cols :].T
    d_ff_input = narrow_rows(matmul_nt(d_gate_b, gate_all) + matmul_nt(d_up_b, up_all))
    d_h_part, grad_ffn = ff_in_back(d_ff_input)
    d_hidden = grad_out + d_h_part
    d_branch, grad_post = attn_back(d_hidden)
    d_branch_rows = widen_rows(d_branch.astype(jnp.bfloat16))
    outw_t = matmul_tn(d_branch_rows, mixed)
    d_mixed = matmul_nt(d_branch_rows, out_all).astype(jnp.bfloat16)
    d_mixed_rows = d_mixed.reshape(seq_length * local_heads, HD)
    delta = jnp.sum(
        d_mixed_rows.astype(jnp.float32) * mixed_rows.astype(jnp.float32), axis=1, keepdims=True
    )
    again = matmul_nt(query_rows, keys_b)
    probs_f = jnp.where(mask_rows, jnp.exp(again - log_total), 0.0)
    d_probs = matmul_nt(d_mixed_rows, values_b)
    d_scores = (probs_f * (d_probs - delta)).astype(jnp.bfloat16)
    d_queries = matmul(d_scores, keys_b).reshape(seq_length, local_heads, HD)
    keys_part = matmul_tn(d_scores, query_rows)
    values_part = matmul_tn(probs_f.astype(jnp.bfloat16), d_mixed_rows)
    d_keys, d_values = (
        lax.psum(keys_part.astype(jnp.bfloat16), "tensor").astype(jnp.float32),
        lax.psum(values_part.astype(jnp.bfloat16), "tensor").astype(jnp.float32),
    )
    d_q_raw, grad_qgain = q_back(d_queries)
    d_k_raw, grad_kgain = k_back(d_keys[:, None, :])
    d_q_b = d_q_raw.reshape(seq_length, local_heads * HD).astype(jnp.bfloat16)
    d_k_b = d_k_raw.reshape(seq_length, HD).astype(jnp.bfloat16)
    d_v_b = d_values.astype(jnp.bfloat16)
    grad_query = matmul_tn(normed_in, d_q_b)
    grad_key = matmul_tn(normed_in, d_k_b)
    grad_value = matmul_tn(normed_in, d_v_b)
    d_normed = matmul_nt(d_q_b, query_all) + kv_share * (
        matmul_nt(d_k_b, key_all) + matmul_nt(d_v_b, value_all)
    )
    d_in_part, grad_pre = in_back(narrow_rows(d_normed))
    inputs_grad = d_hidden + d_in_part
    gain_pre, gain_post, gain_ffn, gain_end, gain_q, gain_k = lax.psum(
        (grad_pre, grad_post, grad_ffn, grad_end, grad_qgain, kv_share * grad_kgain),
        ("dp", "tensor"),
    )
    dp_index = lax.axis_index("dp")
    sent_pre = lax.dynamic_slice_in_dim(gain_pre, dp_index * width_rows, width_rows)
    sent_post = lax.dynamic_slice_in_dim(gain_post, dp_index * width_rows, width_rows)
    sent_ffn = lax.dynamic_slice_in_dim(gain_ffn, dp_index * width_rows, width_rows)
    sent_end = lax.dynamic_slice_in_dim(gain_end, dp_index * width_rows, width_rows)
    sent_qgain = lax.dynamic_slice_in_dim(gain_q, dp_index * head_rows, head_rows)
    sent_kgain = lax.dynamic_slice_in_dim(gain_k, dp_index * head_rows, head_rows)
    query_cols = grad_query.shape[1]
    out_cols = outw_t.shape[1]
    flat_query, flat_key, flat_value, flat_outw = (
        lax.psum_scatter(grad_query.reshape(-1), "dp", scatter_dimension=0, tiled=True),
        lax.psum_scatter(grad_key.reshape(-1), "dp", scatter_dimension=0, tiled=True),
        lax.psum_scatter(grad_value.reshape(-1), "dp", scatter_dimension=0, tiled=True),
        lax.psum_scatter(outw_t.reshape(-1), "dp", scatter_dimension=0, tiled=True),
    )
    sent_query = flat_query.reshape(width_rows, query_cols)
    sent_key = flat_key.reshape(width_rows, HD)
    sent_value = flat_value.reshape(width_rows, HD)
    sent_outw = flat_outw.reshape(width_rows, out_cols).T
    return (
        layer_out,
        inputs_grad,
        sent_pre,
        sent_query,
        sent_key,
        sent_value,
        sent_qgain,
        sent_kgain,
        sent_outw,
        sent_post,
        sent_ffn,
        sent_gate,
        sent_up,
        sent_down,
        sent_end,
    )


def solution(mesh):
    return jax.shard_map(
        on_device,
        mesh=mesh,
        in_specs=(
            P(("dp", "tensor"), None),
            P("dp", None),
            P("dp"),
            P("dp", "tensor"),
            P("dp", None),
            P("dp", None),
            P("dp"),
            P("dp"),
            P("tensor", "dp"),
            P("dp"),
            P("dp"),
            P("dp", "tensor"),
            P("dp", "tensor"),
            P("tensor", "dp"),
            P("dp"),
            P(("dp", "tensor"), None),
        ),
        out_specs=(
            P(("dp", "tensor"), None),
            P(("dp", "tensor"), None),
            P("dp"),
            P("dp", "tensor"),
            P("dp", None),
            P("dp", None),
            P("dp"),
            P("dp"),
            P("tensor", "dp"),
            P("dp"),
            P("dp"),
            P("dp", "tensor"),
            P("dp", "tensor"),
            P("tensor", "dp"),
            P("dp"),
        ),
        check_vma=False,
    )
```

profile of v0, /device:TPU:0, one launch (start us, length us, event | category | flops | bytes accessed | tf_op | source)
XLA Modules:
  0.0 1494.3 jit_solution(17384775213538259779)
XLA Ops:
  16.4 175.6 %all-reduce.15 = (bf16[1152]{0:T(1024)(128)(2,1)S(1)}, bf16[256]{0:T(256)(128)(2,1)S(1)}, bf16[256]{0:T(256)(128)(2,1)S(1)}, bf16[1152]{0:T(1024)(128)(2,1)}) all-reduce(bf16[1152]{0:T(1024)(128)(2,1)S(1)} %dynamic-update-slice, bf16[256]{0:T(256)(128)(2,1)S(1)} %dynamic-update-slice.2, ...), channel_id=1, replica_groups=mesh['dp'=64,'tensor'=2] {'dp'}, use_global_device_ids=true, to_apply=%add.4 | all-reduce | flops 2816 | bytes 11264
  196.8 7.4 all_gather.34
  205.5 3.1 reshape.393
  208.5 2.9 reshape.391
  212.5 1.6 multiply_reduce_fusion.11
  219.8 1.9 fusion.66
  223.4 1.8 multiply_subtract_fusion
  225.2 1.8 copy.79
  227.0 1.8 copy.80
  230.9 2.0 convolution_convert_fusion.1
  232.9 1.8 copy.81
  235.9 3.0 fusion.94
  241.4 16.2 %reduce-scatter.5.cloned.1.call-done = f32[128,1152]{1,0:T(8,128)} async-done(((f32[256,1152]{1,0:T(8,128)}), f32[128,1152]{1,0:T(8,128)}) %reduce-scatter.5.cloned.1.call-update) | async-done | bytes 589840 | tf_op jit(solution)/shard_map/reduce_scatter | solution.py:96
  260.2 156.6 %all-gather.11.cloned.1.call-done = bf16[64,18,10370]{2,1,0:T(8,128)(2,1)} async-done(((bf16[1,18,10370]{2,1,0:T(8,128)(2,1)}), bf16[64,18,10370]{2,1,0:T(8,128)(2,1)}) %all-gather.11.cloned.1.call-update) | async-done | bytes 23892496 | tf_op jit(solution)/shard_map/all_gather | solution.py:28
  416.8 28.7 %reshape.395 = bf16[1152,10370]{1,0:T(8,128)(2,1)} reshape(bf16[64,18,10370]{2,1,0:T(8,128)(2,1)} %all-gather.11.cloned.1.call-done) | data formatting | bytes 47784960
  445.5 2.0 convert_reduce_fusion
  447.7 10.3 all_gather.41
  458.0 7.9 fusion.10
  465.8 3.8 copy-done
  469.6 6.1 multiply_convert_fusion.1
  475.7 5.1 fusion.2
  480.8 22.0 %reduce-scatter.7.cloned.1.call-done = f32[128,1152]{1,0:T(8,128)} async-done(((f32[256,1152]{1,0:T(8,128)}), f32[128,1152]{1,0:T(8,128)}) %reduce-scatter.7.cloned.1.call-update) | async-done | bytes 589840 | tf_op jit(solution)/shard_map/reduce_scatter | solution.py:96
  504.0 1.9 fusion.38
  505.9 2.3 fusion.39
  508.2 9.4 all_gather.42
  517.7 10.4 fusion.18
  530.2 4.1 fusion.4
  534.3 5.1 fusion.21
  539.6 9.8 fusion.97
  549.4 7.8 fusion.95
  557.3 9.0 fusion.96
  566.3 1.9 multiply_reduce_fusion
  568.9 2.2 multiply_reduce_fusion.1
  571.9 8.5 all_gather.43
  581.8 2.2 convolution_convert_fusion.2
  586.7 2.0 fusion.26
  594.5 1.5 fusion.27
  596.0 29.6 %all-reduce.22.cloned.1.call-done = (bf16[256,1,256]{0,2,1:T(8,128)(2,1)}, bf16[256,256]{1,0:T(8,128)(2,1)}) async-done(((bf16[256,1,256]{0,2,1:T(8,128)(2,1)}, bf16[256,256]{1,0:T(8,128)(2,1)}), (bf16[256,1,256]{0,2,1:T(8,128)(2,1)}, bf16[256,256]{1,0:T(8,128)(2,1)})) %all-reduce.22.cloned.1.call-update) | async-done | bytes 262160 | tf_op jit(solution)/shard_map/psum | solution.py:212
  627.8 1.7 fusion.54
  634.0 32.7 %pad_maximum_fusion = f32[1152,10368]{1,0:T(8,128)} fusion(f32[1152,3456]{1,0:T(8,128)} %fusion.97, f32[1152,3456]{1,0:T(8,128)} %fusion.96, f32[1152,3456]{1,0:T(8,128)} %fusion.95), kind=kLoop, calls=%fused_computation | loop fusion | flops 23887872 | bytes 95551488 | tf_op jit(solution)/shard_map/concatenate | solution.py:182
  667.2 2.1 copy.90
  669.9 2.0 copy.93
  672.2 1.6 copy.91
  674.2 1.7 copy.92
  679.4 74.5 %all-reduce.13 = (f32[1152]{0:T(1024)S(1)}, f32[256]{0:T(256)S(1)}, f32[256]{0:T(256)S(1)}, f32[1152]{0:T(1024)S(1)}, f32[1152]{0:T(1024)S(1)}, /*index=5*/f32[1152]{0:T(1024)S(1)}) all-reduce(f32[1152]{0:T(1024)S(1)} %get-tuple-element.25, f32[256]{0:T(256)S(1)} %copy-done.51, ...), channel_id=1, replica_groups=mesh['dp'=64,'tensor'=2] {'dp','tensor'}, use_global_device_ids=true, to_apply=%region_22.23 | all-reduce | flops 5120 | bytes 40960 | tf_op jit(solution)/shard_map/psum | solution.py:228
  757.4 2.1 fusion.41
  759.5 720.0 %all-reduce.20.cloned.1.call-done = (f32[589824]{0:T(1024)}, f32[294912]{0:T(1024)}, f32[294912]{0:T(1024)}, f32[589824]{0:T(1024)}, f32[1152,10368]{1,0:T(8,128)}) async-done(((f32[589824]{0:T(1024)}, f32[294912]{0:T(1024)}, f32[294912]{0:T(1024)}, f32[589824]{0:T(1024)}, f32[1152,10368]{1,0:T(8,128)}), (f32[589824]{0:T(1024)}, f32[294912]{0:T(1024)}, f32[294912]{0:T(1024)}, f32[589824]{0:T(1024)}, ...) | async-done | bytes 54853648
  1485.1 2.5 dynamic-slice_bitcast_fusion
  (237 shorter events, 64.4 us)
Async XLA Ops:
  7.2 198.3 %all-gather.9.cloned.1.call-start = ((), (), s32[]{:S(2)}) async-start(), calls=%async_computation.9 | async-start | bytes 1597440 | tf_op jit(solution)/shard_map/all_gather | solution.py:125
  7.9 200.6 %all-gather.7.cloned.1.call-start = ((), (), s32[]{:S(2)}) async-start(), calls=%async_computation.8 | async-start | bytes 3194880 | tf_op jit(solution)/shard_map/all_gather | solution.py:17
  9.4 248.2 %reduce-scatter.5.cloned.1.call-start = ((), (), s32[]{:S(2)}) async-start(), calls=%async_computation.4 | async-start | bytes 1769472 | tf_op jit(solution)/shard_map/reduce_scatter | solution.py:96
  13.0 206.7 %copy-start.40 = (f32[256]{0:T(256)}, f32[256]{0:T(256)S(1)}, u32[]{:S(2)}) copy-start(f32[256]{0:T(256)S(1)} %convert_element_type.128) | copy-start | bytes 3076
  194.5 35.6 %copy-start.19 = (pred[512,256]{1,0:T(32,128)(4,1)}, pred[512,256]{1,0:T(32,128)(4,1)S(1)}, u32[]{:S(2)}) copy-start(pred[512,256]{1,0:T(32,128)(4,1)S(1)} %reshape.361) | copy-start | bytes 393220
  194.6 16.9 %copy-start.45 = (f32[128]{0:T(128)}, f32[128]{0:T(128)S(1)}, u32[]{:S(2)}) copy-start(f32[128]{0:T(128)S(1)} %multiply_exponential_fusion) | copy-start | bytes 1540
  195.7 15.8 %copy-start.53 = (f32[128]{0:T(128)}, f32[128]{0:T(128)S(1)}, u32[]{:S(2)}) copy-start(f32[128]{0:T(128)S(1)} %fusion.42) | copy-start | bytes 1540
  195.7 15.8 %copy-start.47 = (f32[128]{0:T(128)}, f32[128]{0:T(128)S(1)}, u32[]{:S(2)}) copy-start(f32[128]{0:T(128)S(1)} %fusion.81) | copy-start | bytes 1540
  204.2 9.9 copy-start.2
  218.0 16.7 %copy-start.4 = (f32[256,2,256]{0,2,1:T(8,128)}, f32[256,2,256]{0,2,1:T(8,128)S(1)}, u32[]{:S(2)}) copy-start(f32[256,2,256]{0,2,1:T(8,128)S(1)} %copy.78) | copy-start | bytes 1572868
  222.6 7.5 copy-start.39
  222.6 16.2 %copy-start.32 = (f32[256,2]{0,1:T(2,128)}, f32[256,2]{0,1:T(2,128)S(1)}, u32[]{:S(2)}) copy-start(f32[256,2]{0,1:T(2,128)S(1)} %fusion.79) | copy-start | bytes 6148
  230.2 11.2 copy-start.34
  232.9 8.5 copy-start.50
  232.9 25.9 %copy-start.6 = (bf16[128,1152]{1,0:T(8,128)(2,1)S(1)}, bf16[128,1152]{1,0:T(8,128)(2,1)}, u32[]{:S(2)}) copy-start(bf16[128,1152]{1,0:T(8,128)(2,1)} %param.16) | copy-start | bytes 884740
  235.8 24.4 %copy-start.14 = (bf16[256,512]{1,0:T(8,128)(2,1)}, bf16[256,512]{1,0:T(8,128)(2,1)S(1)}, u32[]{:S(2)}) copy-start(bf16[256,512]{1,0:T(8,128)(2,1)S(1)} %reshape.363) | copy-start | bytes 786436
  238.9 177.9 %all-gather.11.cloned.1.call-start = ((), (), s32[]{:S(2)}) async-start(), calls=%async_computation.10 | async-start | bytes 32747520 | tf_op jit(solution)/shard_map/all_gather | solution.py:28
  241.4 261.4 %reduce-scatter.7.cloned.1.call-start = ((), (), s32[]{:S(2)}) async-start(), calls=%async_computation.5 | async-start | bytes 1769472 | tf_op jit(solution)/shard_map/reduce_scatter | solution.py:96
  241.4 175.4 %copy-start.30 = (f32[1152]{0:T(1024)}, f32[1152]{0:T(1024)S(1)}, u32[]{:S(2)}) copy-start(f32[1152]{0:T(1024)S(1)} %convert_element_type.135) | copy-start | bytes 13828
  258.8 186.7 %copy-start.43 = (f32[128]{0:T(128)}, f32[128]{0:T(128)S(1)}, u32[]{:S(2)}) copy-start(f32[128]{0:T(128)S(1)} %fusion.82) | copy-start | bytes 1540
  260.2 185.3 %copy-start.52 = (f32[128]{0:T(128)}, f32[128]{0:T(128)S(1)}, u32[]{:S(2)}) copy-start(f32[128]{0:T(128)S(1)} %get-tuple-element.47) | copy-start | bytes 1540
  260.2 187.3 %copy-start.46 = (f32[128]{0:T(128)}, f32[128]{0:T(128)S(1)}, u32[]{:S(2)}) copy-start(f32[128]{0:T(128)S(1)} %fusion.83) | copy-start | bytes 1540
  458.0 91.5 %copy-start.8 = (bf16[256,1152]{1,0:T(8,128)(2,1)}, bf16[256,1152]{1,0:T(8,128)(2,1)S(1)}, u32[]{:S(2)}) copy-start(bf16[256,1152]{1,0:T(8,128)(2,1)S(1)} %all_gather.41) | copy-start | bytes 1769476
  458.0 11.6 copy-start
  480.8 85.5 %reduce-scatter.9.cloned.1.call-start = ((), (), s32[]{:S(2)}) async-start(), calls=%async_computation.6 | async-start | bytes 1769472 | tf_op jit(solution)/shard_map/reduce_scatter | solution.py:96
  505.9 22.1 %slice-start = ((s8[24182784]{0:T(1024)(128)(4,1)}), s8[4194304]{0:T(1024)(128)(4,1)S(1)}, s32[]{:S(2)}) async-start(s8[24182784]{0:T(1024)(128)(4,1)} %bitcast.94), calls=%async_computation.13 | async-start | bytes 8388608
  517.6 10.4 copy-start.13
  517.6 10.4 slice-start.1
  517.6 10.4 slice-start.2
  517.6 10.5 slice-start.3
  517.6 11.7 slice-start.4
  517.6 12.6 slice-start.5
  539.4 86.3 %all-reduce.22.cloned.1.call-start = ((), (), s32[]{:S(2)}) async-start(), calls=%async_computation.12 | async-start | bytes 524288 | tf_op jit(solution)/shard_map/psum | solution.py:212
  539.6 9.8 copy-start.21
  549.4 7.8 copy-start.20
  557.3 11.6 copy-start.1
  566.3 14.9 copy-start.12
  571.0 10.7 copy-start.35
  581.7 8.3 copy-start.22
  581.8 9.1 copy-start.5
  581.8 9.1 copy-start.33
  589.9 36.7 %copy-start.41 = (f32[256]{0:T(256)S(1)}, f32[256]{0:T(256)}, u32[]{:S(2)}) copy-start(f32[256]{0:T(256)} %copy-done.40) | copy-start | bytes 3076
  594.5 83.6 %reduce-scatter.11.cloned.1.call-start = ((), (), s32[]{:S(2)}) async-start(), calls=%async_computation.7 | async-start | bytes 1769472 | tf_op jit(solution)/shard_map/reduce_scatter | solution.py:96
  633.7 33.0 %copy-start.3 = (bf16[256,1152]{1,0:T(8,128)(2,1)S(1)}, bf16[256,1152]{1,0:T(8,128)(2,1)}, u32[]{:S(2)}) copy-start(bf16[256,1152]{1,0:T(8,128)(2,1)} %copy-done.2) | copy-start | bytes 1769476
  633.7 33.0 %copy-start.16 = (bf16[256,2,256]{0,2,1:T(8,128)(2,1)S(1)}, bf16[256,2,256]{0,2,1:T(8,128)(2,1)}, u32[]{:S(2)}) copy-start(bf16[256,2,256]{0,2,1:T(8,128)(2,1)} %fusion.44) | copy-start | bytes 786436
  633.7 845.7 %all-reduce.20.cloned.1.call-start = ((), (), s32[]{:S(2)}) async-start(), calls=%async_computation.11 | async-start | bytes 109707264
  676.0 81.5 %copy-start.54 = (f32[128]{0:T(128)S(1)}, f32[128]{0:T(128)}, u32[]{:S(2)}) copy-start(f32[128]{0:T(128)} %copy-done.53) | copy-start | bytes 1540
  676.0 81.5 %copy-start.10 = (f32[128,1152]{1,0:T(8,128)S(1)}, f32[128,1152]{1,0:T(8,128)}, u32[]{:S(2)}) copy-start(f32[128,1152]{1,0:T(8,128)} %copy-done.9) | copy-start | bytes 1769476
  (24 other events, 72.8 us)
Sparse Core Ops, SparseCore 0:
  11.2 69.4 all-gather.8
  84.5 67.4 all-gather.6
  239.0 18.5 reduce-scatter.4
  261.6 155.1 all-gather.10
  480.9 21.8 reduce-scatter.6
  539.5 25.2 reduce-scatter.8
  594.6 31.0 all-reduce.21
  633.8 25.3 reduce-scatter.10
  676.1 803.3 all-reduce.19
where the time goes:
time: 1500 us; the launch traced here: 1490 us
  waiting for transfers between devices  945 us (63%)
  blocking collectives  286 us (19%)
  matrix products  87.8 us (6%)
  local copies, waits for them, and re-layouts  79.7 us (5%)
  other arithmetic  77 us (5%)
  between operations  18.3 us (1%)
    unnamed x10, waiting for transfers between devices  721 us
    unnamed x1, blocking collectives  176 us
    all_gather x1, waiting for transfers between devices, gather_turned(): whole = lax.all_gather(both, axis, axis=0, tiled=True)  157 us
    psum x1, blocking collectives, on_device(): lax.psum((grad_pre, grad_post, grad_ffn, grad_end, grad_qgain, kv_share *...  74.5 us
    unnamed x146, local copies, waits for them, and re-layouts  59 us
    reduce_scatter x4, waiting for transfers between devices, narrow_rows(): lax.psum_scatter(partial_rows, 'tensor', scatter_dimension=0, tiled=True)  38.2 us
    all_gather x4, blocking collectives, widen_rows(): return lax.all_gather(local_rows, 'tensor', axis=0, tiled=True)  35.6 us
    concatenate x1, other arithmetic, on_device(): jnp.concatenate([matmul_tn(ff_input, d_gate_b), matmul_tn(ff_input, d_up_...  32.7 us
  transfers between devices with their start and end apart: 9, of which 5 were waited for; matrix products, arithmetic and copies ran while one was open for 7% of the time, Pallas kernels for 0%

commit v1 on v0

--- a/solution.py
+++ b/solution.py
@@ -25,7 +25,9 @@
     turned = [jnp.moveaxis(a, dim, 0) for a, dim in zip(arrays, dims)]
     widths = [t[0].size for t in turned]
     both = jnp.concatenate([t.reshape(-1, w) for t, w in zip(turned, widths)], axis=1)
-    whole = lax.all_gather(both, axis, axis=0, tiled=True)
+    whole = jnp.concatenate(
+        lax.all_to_all(jnp.stack([both] * lax.axis_size(axis), axis=0), axis, 0, 0), axis=0
+    )
     tiles = jnp.split(whole, [sum(widths[:k]) for k in range(1, len(widths))], axis=1)
     return tuple(
         (

time: 1500 us -> 1790 us (1.19)
  blocking collectives: 286 us -> 678 us
  waiting for transfers between devices: 945 us -> 830 us
    unnamed x1, blocking collectives: 176 us -> 561 us
    all_gather x1 -> x0, waiting for transfers between devices: 157 us -> none  [gather_turned(): whole = lax.all_gather(both, axis, axis=0, tiled=True)]
    reduce_scatter x4, waiting for transfers between devices: 38.2 us -> 78.6 us  [narrow_rows(): lax.psum_scatter(partial_rows, 'tensor', scatter_dimension=0, tiled=True)]
    unnamed x146 -> x175, local copies, waits for them, and re-layouts: 59 us -> 29.4 us
    reshape x0 -> x1, local copies, waits for them, and re-layouts: none -> 28.7 us  [gather_turned(): jnp.concatenate(lax.all_to_all(jnp.stack([both] * lax.axis_size(axis), ax...]
    unnamed x10 -> x9, waiting for transfers between devices: 721 us -> 722 us
  transfers between devices with their start and end apart: 9 -> 9, of which waited for: 5 -> 4; matrix products, arithmetic and copies ran while one was open for 7% -> 6% of each run, Pallas kernels for 0% -> 0%
where the time goes in v1:
time: 1790 us; the launch traced here: 1780 us
  waiting for transfers between devices  830 us (46%)
  blocking collectives  678 us (38%)
  local copies, waits for them, and re-layouts  88.6 us (5%)
  matrix products  83.5 us (5%)
  other arithmetic  70.3 us (4%)
  between operations  18.8 us (1%)
    unnamed x9, waiting for transfers between devices  722 us
    unnamed x1, blocking collectives  561 us
    reduce_scatter x4, waiting for transfers between devices, narrow_rows(): lax.psum_scatter(partial_rows, 'tensor', scatter_dimension=0, tiled=True)  78.6 us
    psum x1, blocking collectives, on_device(): lax.psum((grad_pre, grad_post, grad_ffn, grad_end, grad_qgain, kv_share *...  73.4 us
    all_gather x4, blocking collectives, widen_rows(): return lax.all_gather(local_rows, 'tensor', axis=0, tiled=True)  43.6 us
  transfers between devices with their start and end apart: 9, of which 4 were waited for; matrix products, arithmetic and copies ran while one was open for 6% of the time, Pallas kernels for 0%

profile of v1, /device:TPU:0, one launch (start us, length us, event | category | flops | bytes accessed | tf_op | source)
XLA Modules:
  0.0 1782.3 jit_solution(766103436915816653)
XLA Ops:
  9.9 10.7 stack.2
  20.7 11.7 all-to-all-start
  37.1 561.4 %all-reduce.15 = (bf16[1152]{0:T(1024)(128)(2,1)S(1)}, bf16[256]{0:T(256)(128)(2,1)S(1)}, bf16[256]{0:T(256)(128)(2,1)S(1)}, bf16[1152]{0:T(1024)(128)(2,1)}) all-reduce(bf16[1152]{0:T(1024)(128)(2,1)S(1)} %dynamic-update-slice, bf16[256]{0:T(256)(128)(2,1)S(1)} %dynamic-update-slice.2, ...), channel_id=1, replica_groups=mesh['dp'=64,'tensor'=2] {'dp'}, use_global_device_ids=true, to_apply=%add.4 | all-reduce | flops 2816 | bytes 11264
  601.2 15.8 all_gather.31
  618.2 3.1 reshape.399
  621.3 2.9 reshape.397
  627.2 2.2 multiply_reduce_fusion.10
  630.5 1.8 multiply_subtract_fusion
  632.3 1.8 copy.79
  634.1 1.8 copy.80
  642.3 2.9 fusion.94
  645.3 53.2 %reduce-scatter.5.cloned.1.call-done = f32[128,1152]{1,0:T(8,128)} async-done(((f32[256,1152]{1,0:T(8,128)}), f32[128,1152]{1,0:T(8,128)}) %reduce-scatter.5.cloned.1.call-update) | async-done | bytes 589840 | tf_op jit(solution)/shard_map/reduce_scatter | solution.py:98
  701.1 28.7 %reshape.371 = bf16[1152,10370]{1,0:T(8,128)(2,1)} reshape(bf16[64,18,10370]{2,1,0:T(8,128)(2,1)} %all-to-all-done) | data formatting | bytes 47784960 | tf_op jit(solution)/shard_map/reshape | solution.py:28
  729.8 2.0 convert_reduce_fusion
  732.0 9.9 all_gather.37
  741.9 7.9 fusion.10
  749.7 3.8 copy-done
  753.5 6.0 multiply_convert_fusion.1
  759.6 5.1 fusion.2
  764.7 25.4 %reduce-scatter.7.cloned.1.call-done = f32[128,1152]{1,0:T(8,128)} async-done(((f32[256,1152]{1,0:T(8,128)}), f32[128,1152]{1,0:T(8,128)}) %reduce-scatter.7.cloned.1.call-update) | async-done | bytes 589840 | tf_op jit(solution)/shard_map/reduce_scatter | solution.py:98
  791.3 1.9 fusion.38
  793.2 2.3 fusion.39
  795.5 9.4 all_gather.38
  804.9 10.4 fusion.18
  817.5 4.0 fusion.4
  821.5 5.1 fusion.21
  826.9 9.8 fusion.97
  836.7 7.9 fusion.95
  844.6 9.0 fusion.96
  853.6 1.9 multiply_reduce_fusion
  856.1 2.2 multiply_reduce_fusion.1
  859.2 8.5 all_gather.39
  869.1 2.2 convolution_convert_fusion.2
  872.5 1.5 fusion.25
  874.0 2.0 fusion.26
  880.4 1.5 fusion.44
  881.9 1.5 fusion.27
  883.5 29.6 %all-reduce.22.cloned.1.call-done = (bf16[256,1,256]{0,2,1:T(8,128)(2,1)}, bf16[256,256]{1,0:T(8,128)(2,1)}) async-done(((bf16[256,1,256]{0,2,1:T(8,128)(2,1)}, bf16[256,256]{1,0:T(8,128)(2,1)}), (bf16[256,1,256]{0,2,1:T(8,128)(2,1)}, bf16[256,256]{1,0:T(8,128)(2,1)})) %all-reduce.22.cloned.1.call-update) | async-done | bytes 262160 | tf_op jit(solution)/shard_map/psum | solution.py:214
  915.3 1.7 fusion.54
  921.5 32.7 %pad_maximum_fusion = f32[1152,10368]{1,0:T(8,128)} fusion(f32[1152,3456]{1,0:T(8,128)} %fusion.97, f32[1152,3456]{1,0:T(8,128)} %fusion.96, f32[1152,3456]{1,0:T(8,128)} %fusion.95), kind=kLoop, calls=%fused_computation | loop fusion | flops 23887872 | bytes 95551488 | tf_op jit(solution)/shard_map/concatenate | solution.py:184
  954.7 2.1 copy.90
  957.3 2.0 copy.93
  959.7 1.6 copy.91
  961.7 1.6 copy.92
  966.9 73.4 %all-reduce.13 = (f32[1152]{0:T(1024)S(1)}, f32[256]{0:T(256)S(1)}, f32[256]{0:T(256)S(1)}, f32[1152]{0:T(1024)S(1)}, f32[1152]{0:T(1024)S(1)}, /*index=5*/f32[1152]{0:T(1024)S(1)}) all-reduce(f32[1152]{0:T(1024)S(1)} %get-tuple-element.25, f32[256]{0:T(256)S(1)} %copy-done.61, ...), channel_id=1, replica_groups=mesh['dp'=64,'tensor'=2] {'dp','tensor'}, use_global_device_ids=true, to_apply=%region_22.23 | all-reduce | flops 5120 | bytes 40960 | tf_op jit(solution)/shard_map/psum | solution.py:230
  1043.8 2.1 fusion.41
  1045.9 721.3 %all-reduce.20.cloned.1.call-done = (f32[589824]{0:T(1024)}, f32[294912]{0:T(1024)}, f32[294912]{0:T(1024)}, f32[589824]{0:T(1024)}, f32[1152,10368]{1,0:T(8,128)}) async-done(((f32[589824]{0:T(1024)}, f32[294912]{0:T(1024)}, f32[294912]{0:T(1024)}, f32[589824]{0:T(1024)}, f32[1152,10368]{1,0:T(8,128)}), (f32[589824]{0:T(1024)}, f32[294912]{0:T(1024)}, f32[294912]{0:T(1024)}, f32[589824]{0:T(1024)}, ...) | async-done | bytes 54853648
  1772.8 2.5 dynamic-slice_bitcast_fusion
  (267 shorter events, 53.8 us)
Async XLA Ops:
  20.6 12.6 copy-start.42
  20.6 12.6 copy-start.48
  20.6 12.6 copy-start.49
  20.6 13.4 copy-start.62
  20.6 15.2 copy-start.47
  20.6 15.5 copy-start.68
  20.6 15.7 copy-start.69
  20.6 15.9 copy-start.70
  20.6 16.2 copy-start.71
  20.6 579.2 %copy-start.6 = (bf16[128,1152]{1,0:T(8,128)(2,1)S(1)}, bf16[128,1152]{1,0:T(8,128)(2,1)}, u32[]{:S(2)}) copy-start(bf16[128,1152]{1,0:T(8,128)(2,1)} %param.16) | copy-start | bytes 884740
  20.7 680.5 %all-to-all-start = ((bf16[64,18,10370]{2,1,0:T(8,128)(2,1)}), bf16[64,18,10370]{2,1,0:T(8,128)(2,1)}, u32[]{:S(2)}, u32[]{:S(2)}) async-start(bf16[64,18,10370]{2,1,0:T(8,128)(2,1)} %stack.2), calls=%async_computation.1 | async-start | bytes 64487424 | tf_op jit(solution)/shard_map/all_to_all | solution.py:29
  32.4 585.9 %all-gather.7.cloned.1.call-start = ((), (), s32[]{:S(2)}) async-start(), calls=%async_computation.10 | async-start | bytes 1597440 | tf_op jit(solution)/shard_map/all_gather | solution.py:127
  33.1 588.2 %all-gather.5.cloned.1.call-start = ((), (), s32[]{:S(2)}) async-start(), calls=%async_computation.9 | async-start | bytes 3194880 | tf_op jit(solution)/shard_map/all_gather | solution.py:17
  33.9 664.6 %reduce-scatter.5.cloned.1.call-start = ((), (), s32[]{:S(2)}) async-start(), calls=%async_computation.5 | async-start | bytes 1769472 | tf_op jit(solution)/shard_map/reduce_scatter | solution.py:98
  36.0 585.3 %copy-start.44 = (f32[256]{0:T(256)}, f32[256]{0:T(256)S(1)}, u32[]{:S(2)}) copy-start(f32[256]{0:T(256)S(1)} %convert_element_type.128) | copy-start | bytes 3076
  598.5 37.9 %copy-start.50 = (f32[256]{0:T(256)}, f32[256]{0:T(256)S(1)}, u32[]{:S(2)}) copy-start(f32[256]{0:T(256)S(1)} %convert_element_type.130) | copy-start | bytes 3076
  598.5 31.9 %copy-start.51 = (f32[256]{0:T(256)}, f32[256]{0:T(256)S(1)}, u32[]{:S(2)}) copy-start(f32[256]{0:T(256)S(1)} %convert_element_type.127) | copy-start | bytes 3076
  599.8 21.5 %copy-start.54 = (f32[128]{0:T(128)}, f32[128]{0:T(128)S(1)}, u32[]{:S(2)}) copy-start(f32[128]{0:T(128)S(1)} %multiply_exponential_fusion) | copy-start | bytes 1540
  617.0 22.9 %copy-start.2 = (bf16[256,1152]{1,0:T(8,128)(2,1)}, bf16[256,1152]{1,0:T(8,128)(2,1)S(1)}, u32[]{:S(2)}) copy-start(bf16[256,1152]{1,0:T(8,128)(2,1)S(1)} %all_gather.31) | copy-start | bytes 1769476
  627.2 12.7 copy-start.4
  640.3 59.4 %copy-start.7 = (bf16[128,1152]{1,0:T(8,128)(2,1)S(1)}, bf16[128,1152]{1,0:T(8,128)(2,1)}, u32[]{:S(2)}) copy-start(bf16[128,1152]{1,0:T(8,128)(2,1)} %param.16) | copy-start | bytes 884740
  642.3 87.5 %copy-start.15 = (bf16[256,512]{1,0:T(8,128)(2,1)}, bf16[256,512]{1,0:T(8,128)(2,1)S(1)}, u32[]{:S(2)}) copy-start(bf16[256,512]{1,0:T(8,128)(2,1)S(1)} %reshape.368) | copy-start | bytes 786436
  645.2 144.9 %reduce-scatter.7.cloned.1.call-start = ((), (), s32[]{:S(2)}) async-start(), calls=%async_computation.6 | async-start | bytes 1769472 | tf_op jit(solution)/shard_map/reduce_scatter | solution.py:98
  645.3 55.8 %copy-start.33 = (f32[1152]{0:T(1024)}, f32[1152]{0:T(1024)S(1)}, u32[]{:S(2)}) copy-start(f32[1152]{0:T(1024)S(1)} %convert_element_type.135) | copy-start | bytes 13828
  699.7 30.1 %copy-start.52 = (f32[128]{0:T(128)}, f32[128]{0:T(128)S(1)}, u32[]{:S(2)}) copy-start(f32[128]{0:T(128)S(1)} %fusion.82) | copy-start | bytes 1540
  701.1 28.8 %copy-start.63 = (f32[128]{0:T(128)}, f32[128]{0:T(128)S(1)}, u32[]{:S(2)}) copy-start(f32[128]{0:T(128)S(1)} %get-tuple-element.47) | copy-start | bytes 1540
  701.1 30.8 %copy-start.55 = (f32[128]{0:T(128)}, f32[128]{0:T(128)S(1)}, u32[]{:S(2)}) copy-start(f32[128]{0:T(128)S(1)} %fusion.83) | copy-start | bytes 1540
  741.9 94.8 %copy-start.9 = (bf16[256,1152]{1,0:T(8,128)(2,1)}, bf16[256,1152]{1,0:T(8,128)(2,1)S(1)}, u32[]{:S(2)}) copy-start(bf16[256,1152]{1,0:T(8,128)(2,1)S(1)} %all_gather.37) | copy-start | bytes 1769476
  741.9 11.6 copy-start
  764.6 88.9 %reduce-scatter.9.cloned.1.call-start = ((), (), s32[]{:S(2)}) async-start(), calls=%async_computation.7 | async-start | bytes 1769472 | tf_op jit(solution)/shard_map/reduce_scatter | solution.py:98
  793.2 22.1 %slice-start = ((s8[24182784]{0:T(1024)(128)(4,1)}), s8[4194304]{0:T(1024)(128)(4,1)S(1)}, s32[]{:S(2)}) async-start(s8[24182784]{0:T(1024)(128)(4,1)} %bitcast.93), calls=%async_computation.13 | async-start | bytes 8388608
  804.9 10.4 copy-start.14
  804.9 10.4 slice-start.1
  804.9 10.4 slice-start.2
  804.9 10.4 slice-start.3
  804.9 11.7 slice-start.4
  804.9 12.6 slice-start.5
  826.7 86.4 %all-reduce.22.cloned.1.call-start = ((), (), s32[]{:S(2)}) async-start(), calls=%async_computation.12 | async-start | bytes 524288 | tf_op jit(solution)/shard_map/psum | solution.py:214
  844.6 11.6 copy-start.1
  853.6 14.9 copy-start.13
  858.3 10.8 copy-start.38
  877.3 36.8 %copy-start.45 = (f32[256]{0:T(256)S(1)}, f32[256]{0:T(256)}, u32[]{:S(2)}) copy-start(f32[256]{0:T(256)} %copy-done.44) | copy-start | bytes 3076
  881.9 83.7 %reduce-scatter.11.cloned.1.call-start = ((), (), s32[]{:S(2)}) async-start(), calls=%async_computation.8 | async-start | bytes 1769472 | tf_op jit(solution)/shard_map/reduce_scatter | solution.py:98
  921.2 33.0 %copy-start.3 = (bf16[256,1152]{1,0:T(8,128)(2,1)S(1)}, bf16[256,1152]{1,0:T(8,128)(2,1)}, u32[]{:S(2)}) copy-start(bf16[256,1152]{1,0:T(8,128)(2,1)} %copy-done.2) | copy-start | bytes 1769476
  921.2 33.0 %copy-start.18 = (bf16[256,2,256]{0,2,1:T(8,128)(2,1)S(1)}, bf16[256,2,256]{0,2,1:T(8,128)(2,1)}, u32[]{:S(2)}) copy-start(bf16[256,2,256]{0,2,1:T(8,128)(2,1)} %fusion.44) | copy-start | bytes 786436
  921.2 845.9 %all-reduce.20.cloned.1.call-start = ((), (), s32[]{:S(2)}) async-start(), calls=%async_computation.11 | async-start | bytes 109707264
  963.4 80.4 %copy-start.65 = (f32[128]{0:T(128)S(1)}, f32[128]{0:T(128)}, u32[]{:S(2)}) copy-start(f32[128]{0:T(128)} %copy-done.64) | copy-start | bytes 1540
  963.4 80.4 %copy-start.11 = (f32[128,1152]{1,0:T(8,128)S(1)}, f32[128,1152]{1,0:T(8,128)}, u32[]{:S(2)}) copy-start(f32[128,1152]{1,0:T(8,128)} %copy-done.10) | copy-start | bytes 1769476
  (39 other events, 147.4 us)
Sparse Core Ops, SparseCore 0:
  36.4 391.6 all-gather.6
  431.9 113.3 all-gather.4
  645.4 53.1 reduce-scatter.4
  764.8 25.2 reduce-scatter.6
  826.8 25.2 reduce-scatter.8
  882.0 31.0 all-reduce.21
  921.3 25.2 reduce-scatter.10
  963.6 803.5 all-reduce.19
